TPU v7x, 512 devices: a whole 4x8x8 slice. The times are simulated.
512 devices in a mesh: rep: 16 (over x, z_lo, core), dp: 32 (over y, z_hi).
Axes of the slice: x: 4, y: 8, z: 8 (z_hi: 4, z_lo: 2; z = z_hi * 2 + z_lo), core: 2. Of those that a mesh axis runs over, the one named last changes fastest.
Arguments:
- image_features: bfloat16 [65536, 1408], P(('rep', 'dp')), parts along dimension 0, may hold values from -24 to 24
- text_embed: bfloat16 [65536, 512], P(('rep', 'dp')), parts along dimension 0, may hold values from -24 to 24
- image_head: bfloat16 [22528, 512], P(('rep', 'dp')), parts along dimension 0, may hold values from -1 to 3
- logit_scale: float32 [1], replicated, may hold values from 10 to 40
Outputs:
- image_features_grad: bfloat16 [65536, 1408], P(('rep', 'dp')), parts along dimension 0
- text_embed_grad: bfloat16 [65536, 512], P(('rep', 'dp')), parts along dimension 0
- image_head_grad: float32 [22528, 512], P(('rep', 'dp')), parts along dimension 0
There are 16 independent parts, one for each index of `rep`. A program takes and returns all parts, laid end to end along the dimension named above; an argument that names none is the same for every part. Nothing has to cross between parts.
All inputs are finite; a program needn't handle non-finite values.
Results may differ from a plain program's by a relative error of at most 0.02.
Values may be sent and summed in bfloat16 or wider, within the bound.
No kernel may reach another device: no remote copies, remote signals or barrier semaphores. Data moves between devices by JAX's collectives and lax.ppermute only.
A program may use at most 64 MiB of HBM per device.

v0:
```python
import jax
import jax.numpy as jnp
from jax import lax
from jax.sharding import Mesh
from jax.sharding import PartitionSpec as P

DP = ("dp_0", "dp_1")
REP_DP = ("rep", "dp_0", "dp_1")


def from_everyone(array, axis):
    devices = lax.axis_size(axis)
    return lax.all_to_all(
        jnp.broadcast_to(array[None], (devices, *array.shape)), axis, 0, 0, tiled=True
    )


def joined_along(parts, dim):
    shape = list(parts.shape[1:])
    shape[dim] *= parts.shape[0]
    return jnp.moveaxis(parts, 0, dim).reshape(shape)


def collect(array, axis, dim):
    parts = from_everyone(array, axis)
    return joined_along(parts, dim)


def gathered_by_axis(array, axes, dim):
    if not axes:
        return array
    nearer = lax.all_gather(array, axes[-1], axis=dim, tiled=True)
    return gathered_by_axis(nearer, axes[:-1], dim)


def split_up(array, dim, devices):
    before, after = (array.shape[:dim], array.shape[dim + 1 :])
    return jnp.moveaxis(array.reshape(*before, devices, -1, *after), dim, 0)


def sent_and_summed(array, axis, dim):
    devices = lax.axis_size(axis)
    parts = lax.all_to_all(split_up(array, dim, devices), axis, 0, 0, tiled=True)
    return jnp.sum(parts, axis=0)


def rows_first(arrays, axis, dims):
    turned = [jnp.moveaxis(a, dim, 0) for a, dim in zip(arrays, dims)]
    widths = [t[0].size for t in turned]
    both = jnp.concatenate([t.reshape(-1, w) for t, w in zip(turned, widths)], axis=1)
    result = lax.all_gather(both, axis, axis=0, tiled=True)
    parts = jnp.split(result, [sum(widths[:k]) for k in range(1, len(widths))], axis=1)
    return tuple(
        (
            jnp.moveaxis(b.reshape(-1, *t.shape[1:]), 0, dim)
            for b, t, dim in zip(parts, turned, dims)
        )
    )


def summed_on_arrival(array, axis, dim):
    devices = lax.axis_size(axis)
    parts = lax.all_to_all(split_up(array, dim, devices), axis, 0, 0, tiled=True)
    return jnp.sum(parts.astype(jnp.float32), axis=0)


def unit_rows(embedding):
    inv_norm = lax.rsqrt(jnp.sum(embedding * embedding, axis=1, keepdims=True) + 1e-06)
    return (embedding * inv_norm, inv_norm)


def norm_backward(embedding, inv_norm, upstream):
    inner = jnp.sum(embedding * upstream, axis=1, keepdims=True)
    return (inv_norm * upstream - embedding * (inv_norm * inv_norm * inv_norm) * inner).astype(
        jnp.bfloat16
    )


def tile_logits(logit_mult, left_rows, right_rows):
    product = lax.dot_general(
        left_rows, right_rows, (((1,), (1,)), ((), ())), preferred_element_type=jnp.float32
    )
    return logit_mult * product


def pair_coef(logits, left_lse, right_lse, left_ids, right_ids):
    label = (left_ids[:, None] == right_ids[None, :]).astype(jnp.float32)
    values = (
        jnp.exp(logits - left_lse[:, None]) + jnp.exp(logits - right_lse[None, :]) - 2.0 * label
    )
    return values.astype(jnp.bfloat16)


def local(image_features, text_embed, image_head, logit_scale):
    logit_mult = logit_scale[0]
    row_count = image_features.shape[0]
    batch_total = row_count * lax.axis_size(DP)
    own_ids = lax.axis_index(DP) * row_count + jnp.arange(row_count, dtype=jnp.int32)
    head_full = collect(image_head, DP, 0)
    img_emb = jnp.dot(image_features, head_full, preferred_element_type=jnp.float32)
    img_scaled, img_inv = unit_rows(img_emb)
    img_unit = img_scaled.astype(jnp.bfloat16)
    txt_emb = text_embed.astype(jnp.float32)
    txt_scaled, txt_inv = unit_rows(txt_emb)
    txt_unit = txt_scaled.astype(jnp.bfloat16)
    text_all = gathered_by_axis(txt_unit, DP, 0)
    exp_tile = jnp.exp(tile_logits(logit_mult, img_unit, text_all))
    col_part = jnp.sum(exp_tile, axis=0)
    row_sum, col_part = (jnp.sum(exp_tile, axis=1), col_part)
    row_lse = jnp.log(row_sum)
    col_lse = jnp.log(sent_and_summed(col_part, DP, 0))
    row_all, col_all = rows_first((row_lse, col_lse), DP, (0, 0))
    all_ids = jnp.arange(batch_total, dtype=jnp.int32)
    img_coef = pair_coef(
        tile_logits(logit_mult, img_unit, text_all), row_lse, col_all, own_ids, all_ids
    )
    img_sum = jnp.dot(img_coef, text_all, preferred_element_type=jnp.float32)
    units = lax.all_gather(img_unit, DP, axis=0, tiled=True)
    piece_ids = jnp.arange(units.shape[0], dtype=jnp.int32)
    txt_coef = pair_coef(
        tile_logits(logit_mult, txt_unit, units), col_lse, row_all, own_ids, piece_ids
    )
    txt_sum = jnp.dot(txt_coef, units, preferred_element_type=jnp.float32)
    img_unit_grad = logit_mult * img_sum
    txt_unit_grad = logit_mult * txt_sum
    img_emb_grad = norm_backward(img_emb, img_inv, img_unit_grad)
    text_embed_grad = norm_backward(txt_emb, txt_inv, txt_unit_grad)
    image_features_grad = lax.dot_general(
        img_emb_grad, head_full, (((1,), (1,)), ((), ())), preferred_element_type=jnp.float32
    ).astype(jnp.bfloat16)
    head_partial = lax.dot_general(
        image_features, img_emb_grad, (((0,), (0,)), ((), ())), preferred_element_type=jnp.float32
    )
    image_head_grad = summed_on_arrival(head_partial.astype(jnp.bfloat16), DP, 0)
    return (image_features_grad, text_embed_grad, image_head_grad)


def solution(mesh):
    split = Mesh(mesh.devices.reshape(mesh.shape["rep"], 8, 4), ("rep", "dp_0", "dp_1"))
    return jax.shard_map(
        local,
        mesh=split,
        in_specs=(P(REP_DP, None), P(REP_DP, None), P(REP_DP, None), P()),
        out_specs=(P(REP_DP, None), P(REP_DP, None), P(REP_DP, None)),
        check_vma=False,
    )
```

profile of v0, /device:TPU:6, one launch (start us, length us, event | category | flops | bytes accessed | tf_op | source)
XLA Modules:
  0.0 281.0 jit_solution(6966936409692230886)
XLA Ops:
  7.2 1.1 fusion.9
  8.3 1.0 fusion.10
  9.3 22.3 %all_gather.12 = bf16[512,512]{1,0:T(8,128)(2,1)} all-gather(bf16[128,512]{1,0:T(8,128)(2,1)S(1)} %fusion.10), channel_id=1, replica_groups=mesh['rep'=16,'dp_0'=8,'dp_1'=4] {'dp_1'}, dimensions={0}, use_global_device_ids=true | all-gather | bytes 655360 | tf_op jit(solution)/shard_map/all_gather | solution.py:32
  31.7 1.0 broadcast_in_dim.2
  32.6 64.9 %all_to_all.19 = bf16[32,44,512]{2,1,0:T(8,128)(2,1)S(1)} all-to-all(bf16[32,44,512]{2,1,0:T(8,128)(2,1)S(1)} %broadcast_in_dim.2), channel_id=1, replica_groups=mesh['rep'=16,'dp_0'=8,'dp_1'=4] {'dp_0','dp_1'}, dimensions={0} | all-to-all | bytes 2883584 | tf_op jit(solution)/shard_map/all_to_all | solution.py:13
  97.6 0.3 reshape.67
  97.9 0.5 multiply_reduce_fusion.1
  98.4 0.8 multiply_convert_fusion
  99.8 17.5 %all-gather.3.cloned.1.call-done = bf16[4096,512]{1,0:T(8,128)(2,1)} async-done(((bf16[512,512]{1,0:T(8,128)(2,1)}), bf16[4096,512]{1,0:T(8,128)(2,1)}) %all-gather.3.cloned.1.call-update) | async-done | bytes 4194320 | tf_op jit(solution)/shard_map/all_gather | solution.py:32
  117.3 5.7 %exponential_reduce_fusion.1 = (f32[128]{0:T(128)S(1)}, f32[4096]{0:T(1024)}, f32[128,4096]{1,0:T(8,128)}) fusion(bf16[128,512]{1,0:T(8,128)(2,1)} %multiply_convert_fusion, bf16[4096,512]{1,0:T(8,128)(2,1)} %all-gather.3.cloned.1.call-done, f32[]{:T(128)} %bitcast.24), kind=kOutput, calls=%fused_computation.12 | convolution fusion | flops 538439552 | bytes 6439428 | tf_op jit(solution)/shard_map/dot_general | solution.py:80
  123.0 9.7 %all-to-all-start.1 = ((f32[32,1,128]{2,1,0:T(1,128)}), f32[32,1,128]{2,1,0:T(1,128)S(1)}, u32[]{:S(2)}, u32[]{:S(2)}) async-start(f32[32,1,128]{2,1,0:T(1,128)} %bitcast.2), calls=%async_computation.1 | async-start | bytes 32768 | tf_op jit(solution)/shard_map/all_to_all | solution.py:43
  132.7 12.1 %all-to-all-done.1 = f32[32,1,128]{2,1,0:T(1,128)S(1)} async-done(((f32[32,1,128]{2,1,0:T(1,128)}), f32[32,1,128]{2,1,0:T(1,128)S(1)}, u32[]{:S(2)}, u32[]{:S(2)}) %all-to-all-start.1) | async-done | bytes 16416 | tf_op jit(solution)/shard_map/all_to_all | solution.py:43
  144.9 76.4 %all_gather.14 = f32[4096,2]{0,1:T(2,128)S(1)} all-gather(f32[128,2]{0,1:T(2,128)S(1)} %pad_maximum_fusion), channel_id=1, replica_groups=mesh['rep'=16,'dp_0'=8,'dp_1'=4] {'dp_0','dp_1'}, dimensions={0}, use_global_device_ids=true | all-gather | bytes 33792 | tf_op jit(solution)/shard_map/all_gather | solution.py:51
  221.3 3.9 %multiply_reduce_fusion = (f32[128]{0:T(128)S(1)}, f32[128,512]{1,0:T(8,128)S(1)}) fusion(f32[128,512]{1,0:T(8,128)S(1)} %get-tuple-element.16, bf16[4096,512]{1,0:T(8,128)(2,1)} %all-gather.3.cloned.1.call-done, f32[128,4096]{1,0:T(8,128)} %get-tuple-element.17, s32[128]{0:T(128)S(1)} %iota_add_fusion, f32[4096]{0:T(1024)S(1)} %bitcast.28, ...), kind=kOutput, calls=%fused_computation.31 | convolution fusion | flops 540737408 | bytes 6833668 | tf_op jit(solution)/shard_map/dot_general | solution.py:117
  225.3 0.6 copy-done.2
  226.0 1.7 fusion
  227.6 1.7 copy.10
  229.3 1.3 reshape.68
  230.6 5.2 %all-to-all-start.2 = ((bf16[32,44,512]{2,1,0:T(8,128)(2,1)}), bf16[32,44,512]{2,1,0:T(8,128)(2,1)S(1)}, u32[]{:S(2)}, u32[]{:S(2)}) async-start(bf16[32,44,512]{2,1,0:T(8,128)(2,1)} %reshape.68), calls=%async_computation.2 | async-start | bytes 3145728 | tf_op jit(solution)/shard_map/all_to_all | solution.py:63
  235.9 2.3 convolution_convert_fusion.1
  238.2 28.6 %all-to-all-done.2 = bf16[32,44,512]{2,1,0:T(8,128)(2,1)S(1)} async-done(((bf16[32,44,512]{2,1,0:T(8,128)(2,1)}), bf16[32,44,512]{2,1,0:T(8,128)(2,1)S(1)}, u32[]{:S(2)}, u32[]{:S(2)}) %all-to-all-start.2) | async-done | bytes 1441824 | tf_op jit(solution)/shard_map/all_to_all | solution.py:63
  266.8 0.9 convert_reduce_fusion
  267.7 5.7 %fusion.14 = (f32[128]{0:T(128)S(1)}, f32[128,512]{1,0:T(8,128)S(1)}) fusion(bf16[128,512]{1,0:T(8,128)(2,1)S(1)} %copy-done.1, bf16[4096,512]{1,0:T(8,128)(2,1)} %all-gather.5.cloned.1.call-done, bf16[128,512]{1,0:T(8,128)(2,1)} %copy-done.3, f32[4096]{0:T(1024)S(1)} %bitcast.27, f32[128]{0:T(128)S(1)} %get-tuple-element.9, s32[128]{0:T(128)S(1)} %iota_add_fusion, ...), kind=kOutput, calls=%fused_computation.29 | convolution fusion | flops 1078198144 | bytes 4736516 | tf_op jit(solution)/shard_map/dot_general | solution.py:123
  273.3 0.8 fusion.13
  (21 shorter events, 0.4 us)
Async XLA Ops:
  7.2 90.7 %copy-start = (bf16[128,1408]{1,0:T(8,128)(2,1)S(1)}, bf16[128,1408]{1,0:T(8,128)(2,1)}, u32[]{:S(2)}) copy-start(bf16[128,1408]{1,0:T(8,128)(2,1)} %param.4) | copy-start | bytes 1081348
  7.2 110.1 %all-gather.3.cloned.1.call-start = ((), (), s32[]{:S(2)}) async-start(), calls=%async_computation.3 | async-start | bytes 4718592 | tf_op jit(solution)/shard_map/all_gather | solution.py:32
  9.3 23.3 %copy-start.3 = (bf16[128,512]{1,0:T(8,128)(2,1)}, bf16[128,512]{1,0:T(8,128)(2,1)S(1)}, u32[]{:S(2)}) copy-start(bf16[128,512]{1,0:T(8,128)(2,1)S(1)} %fusion.10) | copy-start | bytes 393220
  31.6 236.1 %all-gather.5.cloned.1.call-start = ((), (), s32[]{:S(2)}) async-start(), calls=%async_computation.4 | async-start | bytes 4325376 | tf_op jit(solution)/shard_map/all_gather | solution.py:118
  123.0 21.8 %all-to-all-start.1 = ((f32[32,1,128]{2,1,0:T(1,128)}), f32[32,1,128]{2,1,0:T(1,128)S(1)}, u32[]{:S(2)}, u32[]{:S(2)}) async-start(f32[32,1,128]{2,1,0:T(1,128)} %bitcast.2), calls=%async_computation.1 | async-start | bytes 32768 | tf_op jit(solution)/shard_map/all_to_all | solution.py:43
  225.3 0.7 copy-start.2
  230.6 36.1 %all-to-all-start.2 = ((bf16[32,44,512]{2,1,0:T(8,128)(2,1)}), bf16[32,44,512]{2,1,0:T(8,128)(2,1)S(1)}, u32[]{:S(2)}, u32[]{:S(2)}) async-start(bf16[32,44,512]{2,1,0:T(8,128)(2,1)} %reshape.68), calls=%async_computation.2 | async-start | bytes 3145728 | tf_op jit(solution)/shard_map/all_to_all | solution.py:63
  235.9 31.8 %copy-start.1 = (bf16[128,512]{1,0:T(8,128)(2,1)S(1)}, bf16[128,512]{1,0:T(8,128)(2,1)}, u32[]{:S(2)}) copy-start(bf16[128,512]{1,0:T(8,128)(2,1)} %param.5) | copy-start | bytes 393220
Sparse Core Ops, SparseCore 0:
  31.7 85.5 all-gather.2
  121.0 101.9 all-gather.4
where the time goes:
time: 281 us
  blocking collectives  164 us (58%)
  waiting for transfers between devices  58.2 us (21%)
  matrix products  19.7 us (7%)
  starting transfers between devices  15 us (5%)
  between operations  14.8 us (5%)
  local copies, waits for them, and re-layouts  4.97 us (2%)
  other arithmetic  4.66 us (2%)
    all_gather x1, blocking collectives, rows_first(): result = lax.all_gather(both, axis, axis=0, tiled=True)  76.4 us
    all_to_all x1, blocking collectives, from_everyone(): lax.all_to_all(jnp.broadcast_to(array[None], (devices, *array.shape)), ax...  64.9 us
    all_to_all x1, waiting for transfers between devices, summed_on_arrival(): lax.all_to_all(split_up(array, dim, devices), axis, 0, 0, tiled=True)  28.6 us
    all_gather x1, blocking collectives, gathered_by_axis(): nearer = lax.all_gather(array, axes[-1], axis=dim, tiled=True)  22.3 us
    all_gather x1, waiting for transfers between devices, gathered_by_axis(): nearer = lax.all_gather(array, axes[-1], axis=dim, tiled=True)  17.5 us
    all_to_all x1, waiting for transfers between devices, sent_and_summed(): lax.all_to_all(split_up(array, dim, devices), axis, 0, 0, tiled=True)  12.1 us
    all_to_all x1, starting transfers between devices, sent_and_summed(): lax.all_to_all(split_up(array, dim, devices), axis, 0, 0, tiled=True)  9.68 us
    dot_general x1, matrix products, tile_logits(): lax.dot_general(left_rows, right_rows, (((1,), (1,)), ((), ())), preferre...  5.75 us
  transfers between devices with their start and end apart: 4, of which 3 were waited for; matrix products, arithmetic and copies ran while one was open for 7% of the time, Pallas kernels for 0%

commit v1 on v0

--- a/solution.py
+++ b/solution.py
@@ -6,6 +6,11 @@
 
 DP = ("dp_0", "dp_1")
 REP_DP = ("rep", "dp_0", "dp_1")
+
+
+def exchange_gather(array, mesh_axis, dim):
+    sent = jnp.stack([array] * lax.axis_size(mesh_axis))
+    return jnp.concatenate(lax.all_to_all(sent, mesh_axis, 0, 0), axis=dim)
 
 
 def from_everyone(array, axis):
@@ -48,7 +53,7 @@
     turned = [jnp.moveaxis(a, dim, 0) for a, dim in zip(arrays, dims)]
     widths = [t[0].size for t in turned]
     both = jnp.concatenate([t.reshape(-1, w) for t, w in zip(turned, widths)], axis=1)
-    result = lax.all_gather(both, axis, axis=0, tiled=True)
+    result = exchange_gather(both, axis, 0)
     parts = jnp.split(result, [sum(widths[:k]) for k in range(1, len(widths))], axis=1)
     return tuple(
         (

time: 281 us -> 270 us (0.961)
  blocking collectives: 164 us -> 87.2 us
  waiting for transfers between devices: 58.2 us -> 120 us
    all_gather x1 -> x0, blocking collectives: 76.4 us -> none  [rows_first(): result = lax.all_gather(both, axis, axis=0, tiled=True)]
    all_gather x1, waiting for transfers between devices: 0.01 us -> 35 us  [local(): units = lax.all_gather(img_unit, DP, axis=0, tiled=True)]
    all_to_all x1, waiting for transfers between devices: 28.6 us -> 42.8 us  [summed_on_arrival(): lax.all_to_all(split_up(array, dim, devices), axis, 0, 0, tiled=True)]
    all_to_all x0 -> x1, waiting for transfers between devices: none -> 12.2 us  [exchange_gather(): return jnp.concatenate(lax.all_to_all(sent, mesh_axis, 0, 0), axis=dim)]
    all_to_all x0 -> x1, starting transfers between devices: none -> 3.85 us  [exchange_gather(): return jnp.concatenate(lax.all_to_all(sent, mesh_axis, 0, 0), axis=dim)]
  transfers between devices with their start and end apart: 4 -> 5, of which waited for: 3 -> 5; matrix products, arithmetic and copies ran while one was open for 7% -> 8% of each run, Pallas kernels for 0% -> 0%
where the time goes in v1:
time: 270 us; the launch traced here: 269 us
  waiting for transfers between devices  120 us (44%)
  blocking collectives  87.2 us (32%)
  matrix products  19.7 us (7%)
  starting transfers between devices  17.6 us (7%)
  between operations  14.8 us (5%)
  local copies, waits for them, and re-layouts  5.61 us (2%)
  other arithmetic  4.66 us (2%)
    all_to_all x1, blocking collectives, from_everyone(): lax.all_to_all(jnp.broadcast_to(array[None], (devices, *array.shape)), ax...  64.9 us
    all_to_all x1, waiting for transfers between devices, summed_on_arrival(): lax.all_to_all(split_up(array, dim, devices), axis, 0, 0, tiled=True)  42.8 us
    all_gather x1, waiting for transfers between devices, local(): units = lax.all_gather(img_unit, DP, axis=0, tiled=True)  35 us
    all_gather x1, blocking collectives, gathered_by_axis(): nearer = lax.all_gather(array, axes[-1], axis=dim, tiled=True)  22.3 us
    all_gather x1, waiting for transfers between devices, gathered_by_axis(): nearer = lax.all_gather(array, axes[-1], axis=dim, tiled=True)  17.5 us
    all_to_all x1, waiting for transfers between devices, exchange_gather(): return jnp.concatenate(lax.all_to_all(sent, mesh_axis, 0, 0), axis=dim)  12.2 us
    all_to_all x1, waiting for transfers between devices, sent_and_summed(): lax.all_to_all(split_up(array, dim, devices), axis, 0, 0, tiled=True)  12.1 us
    all_to_all x1, starting transfers between devices, sent_and_summed(): lax.all_to_all(split_up(array, dim, devices), axis, 0, 0, tiled=True)  9.68 us
  transfers between devices with their start and end apart: 5, of which 5 were waited for; matrix products, arithmetic and copies ran while one was open for 8% of the time, Pallas kernels for 0%

profile of v1, /device:TPU:6, one launch (start us, length us, event | category | flops | bytes accessed | tf_op | source)
XLA Modules:
  0.0 269.2 jit_solution(5607981453867302120)
XLA Ops:
  7.2 1.1 fusion.9
  8.3 1.0 fusion.10
  9.3 22.3 %all_gather.9 = bf16[512,512]{1,0:T(8,128)(2,1)} all-gather(bf16[128,512]{1,0:T(8,128)(2,1)S(1)} %fusion.10), channel_id=1, replica_groups=mesh['rep'=16,'dp_0'=8,'dp_1'=4] {'dp_1'}, dimensions={0}, use_global_device_ids=true | all-gather | bytes 655360 | tf_op jit(solution)/shard_map/all_gather | solution.py:37
  31.7 1.0 broadcast_in_dim.2
  32.6 64.9 %all_to_all.24 = bf16[32,44,512]{2,1,0:T(8,128)(2,1)S(1)} all-to-all(bf16[32,44,512]{2,1,0:T(8,128)(2,1)S(1)} %broadcast_in_dim.2), channel_id=1, replica_groups=mesh['rep'=16,'dp_0'=8,'dp_1'=4] {'dp_0','dp_1'}, dimensions={0} | all-to-all | bytes 2883584 | tf_op jit(solution)/shard_map/all_to_all | solution.py:18
  98.4 0.8 multiply_convert_fusion
  99.8 17.5 %all-gather.3.cloned.1.call-done = bf16[4096,512]{1,0:T(8,128)(2,1)} async-done(((bf16[512,512]{1,0:T(8,128)(2,1)}), bf16[4096,512]{1,0:T(8,128)(2,1)}) %all-gather.3.cloned.1.call-update) | async-done | bytes 4194320 | tf_op jit(solution)/shard_map/all_gather | solution.py:37
  117.3 5.7 %exponential_reduce_fusion.1 = (f32[128]{0:T(128)S(1)}, f32[4096]{0:T(1024)}, f32[128,4096]{1,0:T(8,128)}) fusion(bf16[128,512]{1,0:T(8,128)(2,1)} %multiply_convert_fusion, bf16[4096,512]{1,0:T(8,128)(2,1)} %all-gather.3.cloned.1.call-done, f32[]{:T(128)} %bitcast.25), kind=kOutput, calls=%fused_computation.12 | convolution fusion | flops 538439552 | bytes 6439428 | tf_op jit(solution)/shard_map/dot_general | solution.py:85
  123.0 9.7 %all-to-all-start.1 = ((f32[32,1,128]{2,1,0:T(1,128)}), f32[32,1,128]{2,1,0:T(1,128)S(1)}, u32[]{:S(2)}, u32[]{:S(2)}) async-start(f32[32,1,128]{2,1,0:T(1,128)} %bitcast.2), calls=%async_computation.1 | async-start | bytes 32768 | tf_op jit(solution)/shard_map/all_to_all | solution.py:48
  132.7 12.1 %all-to-all-done.1 = f32[32,1,128]{2,1,0:T(1,128)S(1)} async-done(((f32[32,1,128]{2,1,0:T(1,128)}), f32[32,1,128]{2,1,0:T(1,128)S(1)}, u32[]{:S(2)}, u32[]{:S(2)}) %all-to-all-start.1) | async-done | bytes 16416 | tf_op jit(solution)/shard_map/all_to_all | solution.py:48
  145.5 3.9 %all-to-all-start.2 = ((f32[32,128,2]{1,2,0:T(2,128)}), f32[32,128,2]{1,2,0:T(2,128)S(1)}, u32[]{:S(2)}, u32[]{:S(2)}) async-start(f32[32,128,2]{1,2,0:T(2,128)} %stack.2), calls=%async_computation.2 | async-start | bytes 65536 | tf_op jit(solution)/shard_map/all_to_all | solution.py:13
  149.3 12.2 %all-to-all-done.2 = f32[32,128,2]{1,2,0:T(2,128)S(1)} async-done(((f32[32,128,2]{1,2,0:T(2,128)}), f32[32,128,2]{1,2,0:T(2,128)S(1)}, u32[]{:S(2)}, u32[]{:S(2)}) %all-to-all-start.2) | async-done | bytes 32800 | tf_op jit(solution)/shard_map/all_to_all | solution.py:13
  161.6 3.9 %multiply_reduce_fusion = (f32[128]{0:T(128)S(1)}, f32[128,512]{1,0:T(8,128)S(1)}) fusion(f32[128,512]{1,0:T(8,128)S(1)} %get-tuple-element.16, bf16[4096,512]{1,0:T(8,128)(2,1)} %all-gather.3.cloned.1.call-done, f32[128,4096]{1,0:T(8,128)} %get-tuple-element.17, s32[128]{0:T(128)S(1)} %iota_add_fusion, f32[4096]{0:T(1024)S(1)} %bitcast.30, ...), kind=kOutput, calls=%fused_computation.31 | convolution fusion | flops 540737408 | bytes 6833668 | tf_op jit(solution)/shard_map/dot_general | solution.py:122
  165.6 0.6 copy-done.2
  166.2 1.7 fusion
  167.9 1.7 copy.12
  169.6 1.3 reshape.74
  170.9 4.0 %all-to-all-start.3 = ((bf16[32,44,512]{2,1,0:T(8,128)(2,1)}), bf16[32,44,512]{2,1,0:T(8,128)(2,1)S(1)}, u32[]{:S(2)}, u32[]{:S(2)}) async-start(bf16[32,44,512]{2,1,0:T(8,128)(2,1)} %reshape.74), calls=%async_computation.3 | async-start | bytes 3145728 | tf_op jit(solution)/shard_map/all_to_all | solution.py:68
  174.9 2.3 convolution_convert_fusion.1
  177.2 42.8 %all-to-all-done.3 = bf16[32,44,512]{2,1,0:T(8,128)(2,1)S(1)} async-done(((bf16[32,44,512]{2,1,0:T(8,128)(2,1)}), bf16[32,44,512]{2,1,0:T(8,128)(2,1)S(1)}, u32[]{:S(2)}, u32[]{:S(2)}) %all-to-all-start.3) | async-done | bytes 1441824 | tf_op jit(solution)/shard_map/all_to_all | solution.py:68
  220.0 0.9 convert_reduce_fusion
  220.9 35.0 %all-gather.5.cloned.1.call-done = bf16[4096,512]{1,0:T(8,128)(2,1)} async-done(((bf16[128,512]{1,0:T(8,128)(2,1)}), bf16[4096,512]{1,0:T(8,128)(2,1)}) %all-gather.5.cloned.1.call-update) | async-done | bytes 4194320 | tf_op jit(solution)/shard_map/all_gather | solution.py:123
  255.9 5.7 %fusion.14 = (f32[128]{0:T(128)S(1)}, f32[128,512]{1,0:T(8,128)S(1)}) fusion(bf16[128,512]{1,0:T(8,128)(2,1)S(1)} %copy-done.1, bf16[4096,512]{1,0:T(8,128)(2,1)} %all-gather.5.cloned.1.call-done, bf16[128,512]{1,0:T(8,128)(2,1)} %copy-done.3, f32[4096]{0:T(1024)S(1)} %bitcast.29, f32[128]{0:T(128)S(1)} %get-tuple-element.9, s32[128]{0:T(128)S(1)} %iota_add_fusion, ...), kind=kOutput, calls=%fused_computation.29 | convolution fusion | flops 1078198144 | bytes 4736516 | tf_op jit(solution)/shard_map/dot_general | solution.py:128
  261.6 0.8 fusion.13
  (23 shorter events, 1.7 us)
Async XLA Ops:
  7.2 90.7 %copy-start = (bf16[128,1408]{1,0:T(8,128)(2,1)S(1)}, bf16[128,1408]{1,0:T(8,128)(2,1)}, u32[]{:S(2)}) copy-start(bf16[128,1408]{1,0:T(8,128)(2,1)} %param.4) | copy-start | bytes 1081348
  7.2 110.1 %all-gather.3.cloned.1.call-start = ((), (), s32[]{:S(2)}) async-start(), calls=%async_computation.4 | async-start | bytes 4718592 | tf_op jit(solution)/shard_map/all_gather | solution.py:37
  9.3 23.3 %copy-start.3 = (bf16[128,512]{1,0:T(8,128)(2,1)}, bf16[128,512]{1,0:T(8,128)(2,1)S(1)}, u32[]{:S(2)}) copy-start(bf16[128,512]{1,0:T(8,128)(2,1)S(1)} %fusion.10) | copy-start | bytes 393220
  31.6 224.3 %all-gather.5.cloned.1.call-start = ((), (), s32[]{:S(2)}) async-start(), calls=%async_computation.5 | async-start | bytes 4325376 | tf_op jit(solution)/shard_map/all_gather | solution.py:123
  123.0 21.8 %all-to-all-start.1 = ((f32[32,1,128]{2,1,0:T(1,128)}), f32[32,1,128]{2,1,0:T(1,128)S(1)}, u32[]{:S(2)}, u32[]{:S(2)}) async-start(f32[32,1,128]{2,1,0:T(1,128)} %bitcast.2), calls=%async_computation.1 | async-start | bytes 32768 | tf_op jit(solution)/shard_map/all_to_all | solution.py:48
  145.5 16.1 %all-to-all-start.2 = ((f32[32,128,2]{1,2,0:T(2,128)}), f32[32,128,2]{1,2,0:T(2,128)S(1)}, u32[]{:S(2)}, u32[]{:S(2)}) async-start(f32[32,128,2]{1,2,0:T(2,128)} %stack.2), calls=%async_computation.2 | async-start | bytes 65536 | tf_op jit(solution)/shard_map/all_to_all | solution.py:13
  165.6 0.7 copy-start.2
  170.9 49.1 %all-to-all-start.3 = ((bf16[32,44,512]{2,1,0:T(8,128)(2,1)}), bf16[32,44,512]{2,1,0:T(8,128)(2,1)S(1)}, u32[]{:S(2)}, u32[]{:S(2)}) async-start(bf16[32,44,512]{2,1,0:T(8,128)(2,1)} %reshape.74), calls=%async_computation.3 | async-start | bytes 3145728 | tf_op jit(solution)/shard_map/all_to_all | solution.py:68
  174.9 81.0 %copy-start.1 = (bf16[128,512]{1,0:T(8,128)(2,1)S(1)}, bf16[128,512]{1,0:T(8,128)(2,1)}, u32[]{:S(2)}) copy-start(bf16[128,512]{1,0:T(8,128)(2,1)} %param.5) | copy-start | bytes 393220
Sparse Core Ops, SparseCore 0:
  31.7 85.5 all-gather.2
  121.0 134.8 all-gather.4
